TPU v7x, 128 devices: a whole 4x4x4 slice. The times are simulated.
128 devices in a mesh: fsdp: 8 (over x, core), tensor: 2 (over y_lo), context: 8 (over z, y_hi).
Axes of the slice: x: 4, y: 4 (y_hi: 2, y_lo: 2; y = y_hi * 2 + y_lo), z: 4, core: 2. Of those that a mesh axis runs over, the one named last changes fastest.
Arguments:
- block_input: bfloat16 [16384, 768], P(('fsdp', 'context')), may hold values from -6 to 6
- seq_lengths: int32 [8, 3], P('fsdp'), may hold values from 1 to 1536, 2048 in all within a row
- attn_gain: bfloat16 [768], P('fsdp'), may hold values from 0.5 to 1.5
- qkv_weight: bfloat16 [768, 3, 768], P('fsdp', None, 'tensor'), may hold values from -0.3969283 to 0.3969283
- proj_weight: bfloat16 [768, 768], P('tensor', 'fsdp'), may hold values from -4 to 4
- mlp_gain: bfloat16 [768], P('fsdp'), may hold values from 0.5 to 1.5
- gelu_weight: bfloat16 [768, 2, 1152], P('fsdp', None, 'tensor'), may hold values from -0.21875 to 0.21875
- down_weight: bfloat16 [1152, 768], P('tensor', 'fsdp'), may hold values from -0.1875 to 0.1875
- out_cotangent: bfloat16 [16384, 768], P(('fsdp', 'context')), may hold values from -6 to 6
Outputs:
- block_output: bfloat16 [16384, 768], P(('fsdp', 'context'))
- input_grad: float32 [16384, 768], P(('fsdp', 'context'))
- attngain_grad: float32 [768], P('fsdp')
- qkv_grad: float32 [768, 3, 768], P('fsdp', None, 'tensor')
- proj_grad: float32 [768, 768], P('tensor', 'fsdp')
- mlpgain_grad: float32 [768], P('fsdp')
- gelu_grad: float32 [768, 2, 1152], P('fsdp', None, 'tensor')
- down_grad: float32 [1152, 768], P('tensor', 'fsdp')
All inputs are finite; a program needn't handle non-finite values.
Results may differ from a plain program's by a relative error of at most 0.02.
Values may be sent and summed in bfloat16 or wider, within the bound.
A program may use at most 128 MiB of HBM per device.

v0:
```python
import jax
import jax.numpy as jnp
from jax import lax
from jax.sharding import PartitionSpec as P

HD = 64
EPSILON = 1e-05
THETA = 160000.0
MASKED_LOW = -1e30


def layer_norm(values):
    centre = values - jnp.mean(values, axis=-1, keepdims=True)
    spread = lax.rsqrt(jnp.mean(centre * centre, axis=-1, keepdims=True) + EPSILON)
    return (centre * spread, spread)


def norm_back(grad_out, normed, spread, gain):
    scaled = grad_out * gain
    inner = jnp.mean(scaled, axis=-1, keepdims=True) + normed * jnp.mean(
        scaled * normed, axis=-1, keepdims=True
    )
    return spread * (scaled - inner)


def segments_of(row_ids, lengths):
    ends = jnp.cumsum(lengths)
    segment = jnp.sum((row_ids[:, None] >= ends[None, :]).astype(jnp.int32), axis=1)
    starts = ends - lengths
    picked = segment[:, None] == jnp.arange(lengths.shape[0], dtype=jnp.int32)[None, :]
    begin = jnp.sum(jnp.where(picked, starts[None, :], 0), axis=1)
    return (segment, row_ids - begin)


def rope_tables(positions, head_dim):
    half_dim = head_dim // 2
    exponent = jnp.arange(half_dim, dtype=jnp.float32) * (-2.0 / head_dim)
    frequency = jnp.power(jnp.float32(THETA), exponent)
    angles = positions.astype(jnp.float32)[:, None] * frequency[None, :]
    return (jnp.cos(angles)[:, None, :], jnp.sin(angles)[:, None, :])


def rotate(values, cosine, sine_tab):
    half_dim = values.shape[-1] // 2
    lower_half, upper_half = (values[..., :half_dim], values[..., half_dim:])
    return jnp.concatenate(
        [lower_half * cosine - upper_half * sine_tab, upper_half * cosine + lower_half * sine_tab],
        axis=-1,
    )


def rotate_back(grads, cosine, sine_tab):
    half_dim = grads.shape[-1] // 2
    lower_half, upper_half = (grads[..., :half_dim], grads[..., half_dim:])
    return jnp.concatenate(
        [lower_half * cosine + upper_half * sine_tab, upper_half * cosine - lower_half * sine_tab],
        axis=-1,
    )


def gelu_parts(gate_pre):
    normal_cdf = 0.5 * (1.0 + jax.scipy.special.erf(gate_pre * 0.7071067811865476))
    density = jnp.exp(-0.5 * gate_pre * gate_pre) * 0.3989422804014327
    return (gate_pre * normal_cdf, normal_cdf + gate_pre * density)


def split_count(row_count):
    pieces = 1
    while row_count // pieces > 1024 and row_count % (2 * pieces) == 0:
        pieces = pieces * 2
    return pieces


def over_blocks(step, running, members):
    row_count = members[0].shape[0]
    pieces = split_count(row_count)
    stride = row_count // pieces

    def one_block(counter, current):
        offset = counter * stride
        sliced = tuple((lax.dynamic_slice_in_dim(member, offset, stride, 0) for member in members))
        return step(current, sliced, offset)

    return lax.fori_loop(0, pieces, one_block, running)


def guarded(step):

    def wrapped(running, members, first_row):
        return step(running, members, first_row)

    def folded(running, members, first_row):
        return over_blocks(wrapped, running, members)

    return folded


def on_device(
    block_input,
    seq_lengths,
    attn_gain,
    qkv_weight,
    proj_weight,
    mlp_gain,
    gelu_weight,
    down_weight,
    out_cotangent,
):
    row_count = block_input.shape[0]
    feature_count = block_input.shape[1]
    lengths = seq_lengths[0]
    group_rows = row_count * lax.axis_size("context")
    own_first = lax.axis_index("context") * row_count
    own_rows = own_first + jnp.arange(row_count, dtype=jnp.int32)
    own_segment, positions = segments_of(own_rows, lengths)
    cosine, sine_tab = rope_tables(positions, HD)
    gathered = (
        lax.all_gather(qkv_weight, "fsdp", axis=0, tiled=True),
        lax.all_gather(proj_weight, "fsdp", axis=1, tiled=True),
        lax.all_gather(gelu_weight, "fsdp", axis=0, tiled=True),
        lax.all_gather(down_weight, "fsdp", axis=1, tiled=True),
        lax.all_gather(attn_gain, "fsdp", axis=0, tiled=True),
        lax.all_gather(mlp_gain, "fsdp", axis=0, tiled=True),
    )
    qkv_full, proj_full, gelu_full, down_full, attn_full, mlp_full = gathered
    local_width = qkv_full.shape[2]
    head_count = local_width // HD
    hidden = gelu_full.shape[2]
    attn_scale = attn_full.astype(jnp.float32)
    mlp_scale = mlp_full.astype(jnp.float32)
    inputs = block_input.astype(jnp.float32)
    normed_attn, spread_attn = layer_norm(inputs)
    hidden_attn = (normed_attn * attn_scale).astype(jnp.bfloat16)
    qkv_flat = qkv_full.reshape(feature_count, 3 * local_width)
    projected = jnp.dot(hidden_attn, qkv_flat, preferred_element_type=jnp.float32).reshape(
        row_count, 3, head_count, HD
    )
    query_bf = rotate(projected[:, 0], cosine, sine_tab).astype(jnp.bfloat16)
    key_bf = rotate(projected[:, 1], cosine, sine_tab).astype(jnp.bfloat16)
    value_bf = projected[:, 2].astype(jnp.bfloat16)
    key_flat = key_bf.reshape(row_count, local_width)
    value_flat = value_bf.reshape(row_count, local_width)
    keys_group, values_group = (
        lax.all_gather(key_flat, "context", axis=0, tiled=True),
        lax.all_gather(value_flat, "context", axis=0, tiled=True),
    )
    keys_heads = keys_group.reshape(group_rows, head_count, HD)
    values_heads = values_group.reshape(group_rows, head_count, HD)
    group_segment, unused_pos = segments_of(jnp.arange(group_rows, dtype=jnp.int32), lengths)
    same_group = (own_segment[:, None] == group_segment[None, :])[None]
    fwd_scores = (
        jnp.einsum("qhd,khd->hqk", query_bf, keys_heads, preferred_element_type=jnp.float32) * 0.125
    )
    row_max = jnp.max(jnp.where(same_group, fwd_scores, MASKED_LOW), axis=2)
    denom_sum = jnp.sum(
        jnp.where(same_group, jnp.exp(fwd_scores - row_max[:, :, None]), 0.0), axis=2
    )
    log_total = row_max + jnp.log(denom_sum)
    fwd_weights = jnp.where(same_group, jnp.exp(fwd_scores - log_total[:, :, None]), 0.0).astype(
        jnp.bfloat16
    )
    mixed = jnp.einsum(
        "hqk,khd->qhd", fwd_weights, values_heads, preferred_element_type=jnp.float32
    ).astype(jnp.bfloat16)
    mixed_flat = mixed.reshape(row_count, local_width)
    attn_part = jnp.dot(mixed_flat, proj_full, preferred_element_type=jnp.float32)
    residual = inputs + lax.psum(attn_part, "tensor")
    normed_mlp, spread_mlp = layer_norm(residual)
    hidden_mlp = (normed_mlp * mlp_scale).astype(jnp.bfloat16)
    gelu_flat = gelu_full.reshape(feature_count, 2 * hidden)
    gate_up = jnp.dot(hidden_mlp, gelu_flat, preferred_element_type=jnp.float32).reshape(
        row_count, 2, hidden
    )
    gate_pre, up_pre = (gate_up[:, 0], gate_up[:, 1])
    gelu_val, gelu_slope = gelu_parts(gate_pre)
    activ = (gelu_val * up_pre).astype(jnp.bfloat16)
    mlp_part = jnp.dot(activ, down_full, preferred_element_type=jnp.float32)
    block_output = (
        residual + lax.psum(mlp_part.astype(jnp.bfloat16), "tensor").astype(jnp.float32)
    ).astype(jnp.bfloat16)
    act_grad = jnp.dot(out_cotangent, down_full.T, preferred_element_type=jnp.float32)
    down_grad_t = jnp.dot(out_cotangent.T, activ, preferred_element_type=jnp.float32)
    gate_up_grad = (
        jnp.stack([act_grad * up_pre * gelu_slope, act_grad * gelu_val], axis=1)
        .astype(jnp.bfloat16)
        .reshape(row_count, 2 * hidden)
    )
    gelu_grad = jnp.dot(hidden_mlp.T, gate_up_grad, preferred_element_type=jnp.float32).reshape(
        feature_count, 2, hidden
    )
    mlp_in_grad = lax.psum(
        jnp.dot(gate_up_grad, gelu_flat.T, preferred_element_type=jnp.float32), "tensor"
    )
    mlpgain_grad = jnp.sum(mlp_in_grad * normed_mlp, axis=0)
    resid_grad = out_cotangent.astype(jnp.float32) + norm_back(
        mlp_in_grad, normed_mlp, spread_mlp, mlp_scale
    )
    resid_bf = resid_grad.astype(jnp.bfloat16)
    out_grad = jnp.dot(resid_bf, proj_full.T, preferred_element_type=jnp.float32).astype(
        jnp.bfloat16
    )
    proj_grad_t = jnp.dot(resid_bf.T, mixed_flat, preferred_element_type=jnp.float32)
    out_heads = out_grad.reshape(row_count, head_count, HD)
    delta = jnp.transpose(
        jnp.sum(out_heads.astype(jnp.float32) * mixed.astype(jnp.float32), axis=2)
    )

    def key_terms(members, first_row):
        key_count = members[0].shape[0]
        key_part = members[0].reshape(key_count, head_count, HD)
        value_part = members[1].reshape(key_count, head_count, HD)
        key_segment, unused = segments_of(
            first_row + jnp.arange(key_count, dtype=jnp.int32), lengths
        )
        same_doc = (own_segment[:, None] == key_segment[None, :])[None]
        scores = (
            jnp.einsum("qhd,khd->hqk", query_bf, key_part, preferred_element_type=jnp.float32)
            * 0.125
        )
        weights = jnp.where(same_doc, jnp.exp(scores - log_total[:, :, None]), 0.0)
        prob_grad = jnp.einsum(
            "qhd,khd->hqk", out_heads, value_part, preferred_element_type=jnp.float32
        )
        score_grad = (weights * (prob_grad - delta[:, :, None])).astype(jnp.bfloat16)
        return (key_part, weights, score_grad)

    def owner_step(running, members, first_row):
        query_grad, key_all, value_all = running
        key_part, weights, score_grad = key_terms(members, first_row)
        key_count = key_part.shape[0]
        query_grad = (
            query_grad
            + jnp.einsum("hqk,khd->qhd", score_grad, key_part, preferred_element_type=jnp.float32)
            * 0.125
        )
        key_piece = (
            jnp.einsum(
                "hqk,qhd->khd", score_grad, query_bf, preferred_element_type=jnp.float32
            ).reshape(key_count, local_width)
            * 0.125
        )
        value_piece = jnp.einsum(
            "hqk,qhd->khd",
            weights.astype(jnp.bfloat16),
            out_heads,
            preferred_element_type=jnp.float32,
        ).reshape(key_count, local_width)
        key_all = lax.dynamic_update_slice_in_dim(
            key_all,
            lax.dynamic_slice_in_dim(key_all, first_row, key_count, 0) + key_piece,
            first_row,
            0,
        )
        value_all = lax.dynamic_update_slice_in_dim(
            value_all,
            lax.dynamic_slice_in_dim(value_all, first_row, key_count, 0) + value_piece,
            first_row,
            0,
        )
        return (query_grad, key_all, value_all)

    grad_start = jnp.zeros((row_count, head_count, HD), jnp.float32)
    back_state = (
        grad_start,
        jnp.zeros((group_rows, local_width), jnp.float32),
        jnp.zeros((group_rows, local_width), jnp.float32),
    )
    back_result = guarded(owner_step)(
        back_state,
        (
            lax.all_gather(key_flat, "context", axis=0, tiled=True),
            lax.all_gather(value_flat, "context", axis=0, tiled=True),
        ),
        jnp.int32(0),
    )
    query_grad = back_result[0]
    key_grad, value_grad = (
        lax.psum_scatter(
            back_result[1].astype(jnp.bfloat16), "context", scatter_dimension=0, tiled=True
        ).astype(jnp.float32),
        lax.psum_scatter(
            back_result[2].astype(jnp.bfloat16), "context", scatter_dimension=0, tiled=True
        ).astype(jnp.float32),
    )
    key_grad = key_grad.reshape(row_count, head_count, HD)
    value_grad = value_grad.reshape(row_count, head_count, HD)
    qkv_rows = (
        jnp.stack(
            [
                rotate_back(query_grad, cosine, sine_tab),
                rotate_back(key_grad, cosine, sine_tab),
                value_grad,
            ],
            axis=1,
        )
        .astype(jnp.bfloat16)
        .reshape(row_count, 3 * local_width)
    )
    qkv_grad = jnp.dot(hidden_attn.T, qkv_rows, preferred_element_type=jnp.float32).reshape(
        feature_count, 3, local_width
    )
    attn_in_grad = lax.psum(
        jnp.dot(qkv_rows, qkv_flat.T, preferred_element_type=jnp.float32).astype(jnp.bfloat16),
        "tensor",
    ).astype(jnp.float32)
    attngain_grad = jnp.sum(attn_in_grad * normed_attn, axis=0)
    input_grad = resid_grad + norm_back(attn_in_grad, normed_attn, spread_attn, attn_scale)
    grads = (
        attngain_grad[:, None],
        mlpgain_grad[:, None],
        qkv_grad.reshape(feature_count, 3 * local_width),
        gelu_grad.reshape(feature_count, 2 * hidden),
        proj_grad_t,
        down_grad_t,
    )
    widths = [g.shape[1] for g in grads]
    packed = jnp.concatenate(grads, axis=1)
    packed = lax.psum_scatter(packed, "fsdp", scatter_dimension=0, tiled=True)
    packed = lax.psum(packed, "context")
    pieces = []
    start = 0
    for width in widths:
        pieces.append(packed[:, start : start + width])
        start += width
    shard_rows = packed.shape[0]
    shares = (
        pieces[0][:, 0],
        pieces[2].reshape(shard_rows, 3, local_width),
        pieces[4].T,
        pieces[1][:, 0],
        pieces[3].reshape(shard_rows, 2, hidden),
        pieces[5].T,
    )
    return (
        block_output,
        input_grad,
        shares[0],
        shares[1],
        shares[2],
        shares[3],
        shares[4],
        shares[5],
    )


def solution(mesh):
    in_specs = (
        P(("fsdp", "context"), None),
        P("fsdp", None),
        P("fsdp"),
        P("fsdp", None, "tensor"),
        P("tensor", "fsdp"),
        P("fsdp"),
        P("fsdp", None, "tensor"),
        P("tensor", "fsdp"),
        P(("fsdp", "context"), None),
    )
    out_specs = (
        P(("fsdp", "context"), None),
        P(("fsdp", "context"), None),
        P("fsdp"),
        P("fsdp", None, "tensor"),
        P("tensor", "fsdp"),
        P("fsdp"),
        P("fsdp", None, "tensor"),
        P("tensor", "fsdp"),
    )
    return jax.shard_map(
        on_device, mesh=mesh, in_specs=in_specs, out_specs=out_specs, check_vma=False
    )
```

profile of v0, /device:TPU:0, one launch (start us, length us, event | category | flops | bytes accessed | tf_op | source)
XLA Modules:
  0.0 698.4 jit_solution(5407401806397029626)
XLA Ops:
  11.6 14.7 %all-reduce.2 = (bf16[768]{0:T(1024)(128)(2,1)S(1)}, bf16[768]{0:T(1024)(128)(2,1)S(1)}) all-reduce(bf16[768]{0:T(1024)(128)(2,1)S(1)} %dynamic-update-slice, bf16[768]{0:T(1024)(128)(2,1)S(1)} %dynamic-update-slice.1), channel_id=1, replica_groups=mesh['fsdp'=8,'tensor'=2,'context'=8] {'fsdp'}, use_global_device_ids=true, to_apply=%add | all-reduce | flops 1536 | bytes 6144
  30.6 6.5 all-gather.5.cloned.1.call-done
  37.1 2.6 copy.52
  42.6 1.7 slice.139
  45.6 13.2 %all_gather.30 = bf16[384,768]{0,1:T(8,128)(2,1)S(1)} all-gather(bf16[384,96]{0,1:T(8,128)(2,1)S(1)} %copy-done.46), channel_id=1, replica_groups=mesh['fsdp'=8,'tensor'=2,'context'=8] {'fsdp'}, dimensions={1}, use_global_device_ids=true | all-gather | bytes 663552 | tf_op jit(solution)/shard_map/all_gather | solution.py:119
  58.8 33.9 %all-gather.9.cloned.1.call-done = bf16[2048,384]{0,1:T(8,128)(2,1)} async-done(((bf16[256,384]{0,1:T(8,128)(2,1)}), bf16[2048,384]{0,1:T(8,128)(2,1)}) %all-gather.9.cloned.1.call-update) | async-done | bytes 1572880 | tf_op jit(solution)/shard_map/all_gather | solution.py:144
  92.7 3.9 select_reduce_fusion.1
  96.6 3.9 select_reduce_fusion
  101.1 42.2 %all-gather.7.cloned.1.call-done = bf16[2048,384]{0,1:T(8,128)(2,1)} async-done(((bf16[256,384]{0,1:T(8,128)(2,1)}), bf16[2048,384]{0,1:T(8,128)(2,1)}) %all-gather.7.cloned.1.call-update) | async-done | bytes 1572880 | tf_op jit(solution)/shard_map/all_gather | solution.py:145
  143.3 7.7 %fusion.13 = bf16[6,64,256]{2,1,0:T(8,128)(2,1)S(1)} fusion(bf16[2048,6,64]{0,2,1:T(8,128)(2,1)} %bitcast.184, f32[6,256,2048]{2,1,0:T(8,128)} %copy-done.7, f32[6,256]{1,0:T(8,128)S(1)} %log_add_fusion, pred[256,2048]{1,0:T(8,128)(4,1)S(1)} %broadcast_compare_fusion.1), kind=kOutput, calls=%fused_computation.37 | convolution fusion | flops 415334400 | bytes 14882816 | tf_op jit(solution)/shard_map/hqk,khd->qhd/dot_general | solution.py:162
  152.4 16.8 %all_gather.33 = bf16[576,768]{0,1:T(8,128)(2,1)} all-gather(bf16[576,96]{0,1:T(8,128)(2,1)S(1)} %copy-done.45), channel_id=1, replica_groups=mesh['fsdp'=8,'tensor'=2,'context'=8] {'fsdp'}, dimensions={1}, use_global_device_ids=true | all-gather | bytes 995328 | tf_op jit(solution)/shard_map/all_gather | solution.py:121
  170.0 2.7 copy.54
  172.7 40.8 %all-reduce.9.cloned.1.call-done = f32[256,768]{1,0:T(8,128)} async-done(((f32[256,768]{1,0:T(8,128)}), f32[256,768]{1,0:T(8,128)}) %all-reduce.9.cloned.1.call-update) | async-done | bytes 786448 | tf_op jit(solution)/shard_map/psum | solution.py:167
  217.8 1.7 convolution_bitcast_fusion.1
  219.8 41.8 %all-reduce.11.cloned.1.call-done = f32[256,768]{1,0:T(8,128)} async-done(((f32[256,768]{1,0:T(8,128)}), f32[256,768]{1,0:T(8,128)}) %all-reduce.11.cloned.1.call-update) | async-done | bytes 786448 | tf_op jit(solution)/shard_map/psum | solution.py:191
  261.6 2.1 multiply_reduce_fusion
  263.8 1.4 multiply_add_fusion
  266.4 2.1 broadcast.210
  268.5 2.0 broadcast.210.clone
  270.5 40.4 %while.20 = (s32[]{:T(128)}, f32[256,6,64]{0,2,1:T(8,128)}, f32[2048,384]{0,1:T(8,128)}, f32[2048,384]{0,1:T(8,128)}, bf16[2048,384]{0,1:T(8,128)(2,1)}, /*index...) while((s32[]{:T(128)}, f32[256,6,64]{0,2,1:T(8,128)}, ...), condition=%wide.region_19.20_spmd.clone, body=%wide.region_17.19_spmd.clone.sunk | while | flops 1024107520 | bytes 131182336 | solution.py:84
  273.2 1.8 constant_dynamic-slice_fusion.5
  275.0 3.3 fusion.105
  278.4 2.6 fusion.106
  281.0 4.3 fusion.107
  288.1 1.7 copy-done.3
  293.4 1.8 constant_dynamic-slice_fusion.5
  295.2 3.3 fusion.105
  298.6 2.7 fusion.106
  301.2 4.3 fusion.107
  308.3 1.7 copy-done.3
  310.9 3.4 convert_element_type.160
  314.4 1.4 convert_element_type.161
  318.9 2.7 fusion.48
  321.6 67.5 %reduce-scatter.4.cloned.1.call-done = bf16[256,384]{0,1:T(8,128)(2,1)} async-done(((bf16[2048,384]{0,1:T(8,128)(2,1)}), bf16[256,384]{0,1:T(8,128)(2,1)}) %reduce-scatter.4.cloned.1.call-update) | async-done | bytes 196624 | tf_op jit(solution)/shard_map/reduce_scatter | solution.py:278
  391.1 74.7 %reduce-scatter.6.cloned.1.call-done = bf16[256,384]{0,1:T(8,128)(2,1)} async-done(((bf16[2048,384]{0,1:T(8,128)(2,1)}), bf16[256,384]{0,1:T(8,128)(2,1)}) %reduce-scatter.6.cloned.1.call-update) | async-done | bytes 196624 | tf_op jit(solution)/shard_map/reduce_scatter | solution.py:281
  467.6 1.5 convolution_convert_fusion
  469.1 3.0 convolution_bitcast_fusion
  472.3 1.4 fusion.38
  473.7 2.6 fusion.45
  476.3 32.8 %all-reduce.15.cloned.1.call-done = (bf16[256,768]{1,0:T(8,128)(2,1)}, bf16[256,768]{1,0:T(8,128)(2,1)}) async-done(((bf16[256,768]{1,0:T(8,128)(2,1)}, bf16[256,768]{1,0:T(8,128)(2,1)}), (bf16[256,768]{1,0:T(8,128)(2,1)}, bf16[256,768]{1,0:T(8,128)(2,1)})) %all-reduce.15.cloned.1.call-update) | async-done | bytes 786448 | tf_op jit(solution)/shard_map/psum | solution.py:179
  509.1 1.4 fusion.27
  510.7 13.5 %concatenate.21 = f32[768,3266]{1,0:T(8,128)} concatenate(f32[768,1]{1,0:T(8,128)S(1)} %broadcast_in_dim.141, f32[768,1]{1,0:T(8,128)S(1)} %broadcast_in_dim.142, f32[768,1152]{1,0:T(8,128)} %fusion.45, f32[768,1152]{1,0:T(8,128)} %fusion.48, f32[768,384]{1,0:T(8,128)} %fusion.38, f32[768,576]{1,0:T(8,128)} %convolution_bitcast_fusion), dimensions={1} | concatenate | bytes 20066304 | tf_op jit(solution)/shard_map/concatenate | solution.py:317
  524.3 62.2 %reduce-scatter.8.cloned.1.call-done = f32[96,3266]{1,0:T(8,128)} async-done(((f32[768,3266]{1,0:T(8,128)}), f32[96,3266]{1,0:T(8,128)}) %reduce-scatter.8.cloned.1.call-update) | async-done | bytes 1254160 | tf_op jit(solution)/shard_map/reduce_scatter | solution.py:318
  588.6 94.9 %all-reduce.13.cloned.1.call-done = f32[96,3266]{1,0:T(8,128)} async-done(((f32[96,3266]{1,0:T(8,128)}), f32[96,3266]{1,0:T(8,128)}) %all-reduce.13.cloned.1.call-update) | async-done | bytes 1254160 | tf_op jit(solution)/shard_map/psum | solution.py:319
  683.4 1.5 fusion.50
  686.8 1.6 slice_reduce_fusion
  688.4 1.7 slice_bitcast_fusion.5
  690.1 1.8 slice_bitcast_fusion.4
  (248 shorter events, 44.2 us)
Async XLA Ops:
  7.2 32.6 %copy-start.10 = (bf16[256,768]{1,0:T(8,128)(2,1)S(1)}, bf16[256,768]{1,0:T(8,128)(2,1)}, u32[]{:S(2)}) copy-start(bf16[256,768]{1,0:T(8,128)(2,1)} %param.11) | copy-start | bytes 1179652
  7.2 29.9 %all-gather.5.cloned.1.call-start = ((), (), s32[]{:S(2)}) async-start(), calls=%async_computation.3 | async-start | bytes 1990656 | tf_op jit(solution)/shard_map/all_gather | solution.py:118
  7.9 84.8 %all-gather.9.cloned.1.call-start = ((), (), s32[]{:S(2)}) async-start(), calls=%async_computation.5 | async-start | bytes 1769472 | tf_op jit(solution)/shard_map/all_gather | solution.py:144
  30.3 10.2 %copy-start.50 = (f32[256]{0:T(256)}, f32[256]{0:T(256)S(1)}, u32[]{:S(2)}) copy-start(f32[256]{0:T(256)S(1)} %add_rsqrt_fusion.1) | copy-start | bytes 3076
  30.6 11.1 %copy-start.40 = (f32[256,32]{0,1:T(8,128)}, f32[256,32]{0,1:T(8,128)S(1)}, u32[]{:S(2)}) copy-start(f32[256,32]{0,1:T(8,128)S(1)} %get-tuple-element.417) | copy-start | bytes 98308
  30.6 11.1 %copy-start.41 = (f32[256,32]{0,1:T(8,128)}, f32[256,32]{0,1:T(8,128)S(1)}, u32[]{:S(2)}) copy-start(f32[256,32]{0,1:T(8,128)S(1)} %get-tuple-element.418) | copy-start | bytes 98308
  39.7 4.6 copy-start.44
  41.6 4.1 copy-start.46
  41.8 54.8 %copy-start.33 = (bf16[256,6,32]{0,2,1:T(8,128)(2,1)}, bf16[256,6,32]{0,2,1:T(8,128)(2,1)S(1)}, u32[]{:S(2)}) copy-start(bf16[256,6,32]{0,2,1:T(8,128)(2,1)S(1)} %get-tuple-element.409) | copy-start | bytes 294916
  41.8 54.8 %copy-start.35 = (bf16[256,6,32]{0,2,1:T(8,128)(2,1)}, bf16[256,6,32]{0,2,1:T(8,128)(2,1)S(1)}, u32[]{:S(2)}) copy-start(bf16[256,6,32]{0,2,1:T(8,128)(2,1)S(1)} %get-tuple-element.410) | copy-start | bytes 294916
  42.5 100.8 %all-gather.7.cloned.1.call-start = ((), (), s32[]{:S(2)}) async-start(), calls=%async_computation.4 | async-start | bytes 1769472 | tf_op jit(solution)/shard_map/all_gather | solution.py:145
  44.3 125.7 %all-gather.11.cloned.1.call-start = ((), (), s32[]{:S(2)}) async-start(), calls=%async_computation.7 | async-start | bytes 2211840 | tf_op jit(solution)/shard_map/all_gather | solution.py:120
  45.1 168.4 %all-reduce.9.cloned.1.call-start = ((), (), s32[]{:S(2)}) async-start(), calls=%async_computation.6 | async-start | bytes 1572864 | tf_op jit(solution)/shard_map/psum | solution.py:167
  58.8 92.1 %copy-start.19 = (bf16[384,768]{0,1:T(8,128)(2,1)}, bf16[384,768]{0,1:T(8,128)(2,1)S(1)}, u32[]{:S(2)}) copy-start(bf16[384,768]{0,1:T(8,128)(2,1)S(1)} %all_gather.30) | copy-start | bytes 1769476
  96.6 4.5 copy-start.7
  101.1 49.8 %copy-start.58 = (f32[6,256]{1,0:T(8,128)}, f32[6,256]{1,0:T(8,128)S(1)}, u32[]{:S(2)}) copy-start(f32[6,256]{1,0:T(8,128)S(1)} %log_add_fusion) | copy-start | bytes 18436
  143.3 9.1 %copy-start.45 = (bf16[576,96]{0,1:T(8,128)(2,1)S(1)}, bf16[576,96]{0,1:T(8,128)(2,1)}, u32[]{:S(2)}) copy-start(bf16[576,96]{0,1:T(8,128)(2,1)} %param.18) | copy-start | bytes 331780
  152.3 109.3 %all-reduce.11.cloned.1.call-start = ((), (), s32[]{:S(2)}) async-start(), calls=%async_computation.8 | async-start | bytes 1572864 | tf_op jit(solution)/shard_map/psum | solution.py:191
  172.7 44.1 %copy-start.31 = (bf16[256,768]{1,0:T(8,128)(2,1)S(1)}, bf16[256,768]{1,0:T(8,128)(2,1)}, u32[]{:S(2)}) copy-start(bf16[256,768]{1,0:T(8,128)(2,1)} %param.19) | copy-start | bytes 1179652
  214.9 48.9 %copy-start.8 = (f32[256,768]{1,0:T(8,128)}, f32[256,768]{1,0:T(8,128)S(1)}, u32[]{:S(2)}) copy-start(f32[256,768]{1,0:T(8,128)S(1)} %get-tuple-element.396) | copy-start | bytes 2359300
  217.5 46.2 %copy-start.42 = (bf16[256,1,576]{0,2,1:T(8,128)(2,1)}, bf16[256,1,576]{0,2,1:T(8,128)(2,1)S(1)}, u32[]{:S(2)}) copy-start(bf16[256,1,576]{0,2,1:T(8,128)(2,1)S(1)} %get-tuple-element.399) | copy-start | bytes 884740
  217.5 46.2 %copy-start.43 = (bf16[256,1,576]{0,2,1:T(8,128)(2,1)}, bf16[256,1,576]{0,2,1:T(8,128)(2,1)S(1)}, u32[]{:S(2)}) copy-start(bf16[256,1,576]{0,2,1:T(8,128)(2,1)S(1)} %get-tuple-element.400) | copy-start | bytes 884740
  217.5 44.1 %copy-start.48 = (f32[256]{0:T(256)S(1)}, f32[256]{0:T(256)}, u32[]{:S(2)}) copy-start(f32[256]{0:T(256)} %copy-done.47) | copy-start | bytes 3076
  217.5 44.1 %copy-start.53 = (f32[256]{0:T(256)S(1)}, f32[256]{0:T(256)}, u32[]{:S(2)}) copy-start(f32[256]{0:T(256)} %copy-done.52) | copy-start | bytes 3076
  217.8 45.9 %copy-start.32 = (bf16[256,768]{1,0:T(8,128)(2,1)S(1)}, bf16[256,768]{1,0:T(8,128)(2,1)}, u32[]{:S(2)}) copy-start(bf16[256,768]{1,0:T(8,128)(2,1)} %param.19) | copy-start | bytes 1179652
  219.6 45.6 %copy-start.20 = (bf16[384,768]{0,1:T(8,128)(2,1)S(1)}, bf16[384,768]{0,1:T(8,128)(2,1)}, u32[]{:S(2)}) copy-start(bf16[384,768]{0,1:T(8,128)(2,1)} %copy-done.19) | copy-start | bytes 1769476
  219.6 169.6 %reduce-scatter.4.cloned.1.call-start = ((), (), s32[]{:S(2)}) async-start(), calls=%async_computation.9 | async-start | bytes 1769472 | tf_op jit(solution)/shard_map/reduce_scatter | solution.py:278
  265.2 5.4 copy-start.15
  272.9 5.5 copy-start.1
  273.2 5.2 copy-start.17
  281.0 5.4 copy-start.4
  293.0 5.5 copy-start.1
  293.4 5.2 copy-start.17
  301.2 5.4 copy-start.4
  310.9 3.5 copy-start.6
  314.4 151.4 %reduce-scatter.6.cloned.1.call-start = ((), (), s32[]{:S(2)}) async-start(), calls=%async_computation.10 | async-start | bytes 1769472 | tf_op jit(solution)/shard_map/reduce_scatter | solution.py:281
  315.9 193.2 %all-reduce.15.cloned.1.call-start = ((), (), s32[]{:S(2)}) async-start(), calls=%async_computation.13 | async-start | bytes 1572864 | tf_op jit(solution)/shard_map/psum | solution.py:179
  318.9 71.2 %copy-start.14 = (f32[256,6,64]{0,2,1:T(8,128)S(1)}, f32[256,6,64]{0,2,1:T(8,128)}, u32[]{:S(2)}) copy-start(f32[256,6,64]{0,2,1:T(8,128)} %get-tuple-element.285) | copy-start | bytes 1179652
  318.9 148.7 %copy-start.13 = (bf16[768,3,384]{0,2,1:T(8,128)(2,1)S(1)}, bf16[768,3,384]{0,2,1:T(8,128)(2,1)}, u32[]{:S(2)}) copy-start(bf16[768,3,384]{0,2,1:T(8,128)(2,1)} %copy-done.12) | copy-start | bytes 5308420
  466.8 5.3 copy-start.55
  467.6 4.7 copy-start.16
  469.0 4.7 copy-start.11
  469.0 4.7 copy-start.22
  469.0 4.7 copy-start.51
  469.1 117.4 %reduce-scatter.8.cloned.1.call-start = ((), (), s32[]{:S(2)}) async-start(), calls=%async_computation.11 | async-start | bytes 11501568 | tf_op jit(solution)/shard_map/reduce_scatter | solution.py:318
  524.2 62.3 %copy-start.39 = (bf16[256,768]{1,0:T(8,128)(2,1)S(1)}, bf16[256,768]{1,0:T(8,128)(2,1)}, u32[]{:S(2)}) copy-start(bf16[256,768]{1,0:T(8,128)(2,1)} %get-tuple-element.393) | copy-start | bytes 1179652
  524.2 63.2 %copy-start.30 = (bf16[256,768]{1,0:T(8,128)(2,1)S(1)}, bf16[256,768]{1,0:T(8,128)(2,1)}, u32[]{:S(2)}) copy-start(bf16[256,768]{1,0:T(8,128)(2,1)} %get-tuple-element.394) | copy-start | bytes 1179652
  524.3 159.2 %all-reduce.13.cloned.1.call-start = ((), (), s32[]{:S(2)}) async-start(), calls=%async_computation.12 | async-start | bytes 2555904 | tf_op jit(solution)/shard_map/psum | solution.py:319
  (41 other events, 95.8 us)
Sparse Core Ops, SparseCore 0:
  9.7 27.3 all-gather.4
  42.7 50.0 all-gather.8
  95.5 47.7 all-gather.6
  145.4 24.5 all-gather.10
  172.8 40.5 all-reduce.8
  219.7 41.8 all-reduce.10
  314.5 74.6 reduce-scatter.3
  393.3 72.4 reduce-scatter.5
  469.2 39.8 all-reduce.14
  524.4 62.0 reduce-scatter.7
  589.2 94.2 all-reduce.12
where the time goes:
time: 700 us; the launch traced here: 698 us
  waiting for transfers between devices  499 us (71%)
  matrix products  54.2 us (8%)
  local copies, waits for them, and re-layouts  54.1 us (8%)
  blocking collectives  44.7 us (6%)
  other arithmetic  30.3 us (4%)
  between operations  15.2 us (2%)
    psum x1, waiting for transfers between devices, on_device(): packed = lax.psum(packed, 'context')  94.9 us
    reduce_scatter x1, waiting for transfers between devices, on_device(): lax.psum_scatter(back_result[2].astype(jnp.bfloat16), 'context', scatter_...  74.7 us
    reduce_scatter x1, waiting for transfers between devices, on_device(): lax.psum_scatter(back_result[1].astype(jnp.bfloat16), 'context', scatter_...  67.5 us
    reduce_scatter x1, waiting for transfers between devices, on_device(): packed = lax.psum_scatter(packed, 'fsdp', scatter_dimension=0, tiled=True)  62.2 us
    all_gather x1, waiting for transfers between devices, on_device(): lax.all_gather(value_flat, 'context', axis=0, tiled=True)  42.2 us
    psum x1, waiting for transfers between devices, on_device(): lax.psum(jnp.dot(gate_up_grad, gelu_flat.T, preferred_element_type=jnp.fl...  41.8 us
    psum x1, waiting for transfers between devices, on_device(): residual = inputs + lax.psum(attn_part, 'tensor')  40.8 us
    all_gather x1, waiting for transfers between devices, on_device(): lax.all_gather(key_flat, 'context', axis=0, tiled=True)  33.9 us
  transfers between devices with their start and end apart: 11, of which 11 were waited for; matrix products, arithmetic and copies ran while one was open for 7% of the time, Pallas kernels for 0%

commit v1 on v0

--- a/solution.py
+++ b/solution.py
@@ -316,7 +316,7 @@
     widths = [g.shape[1] for g in grads]
     packed = jnp.concatenate(grads, axis=1)
     packed = lax.psum_scatter(packed, "fsdp", scatter_dimension=0, tiled=True)
-    packed = lax.psum(packed, "context")
+    packed = jnp.sum(lax.all_gather(packed, "context"), axis=0)
     pieces = []
     start = 0
     for width in widths:

time: 700 us -> 730 us (1.043)
  waiting for transfers between devices: 499 us -> 528 us
    all_gather x0 -> x1, waiting for transfers between devices: none -> 124 us  [on_device(): packed = jnp.sum(lax.all_gather(packed, 'context'), axis=0)]
    psum x1 -> x0, waiting for transfers between devices: 94.9 us -> none  [on_device(): packed = lax.psum(packed, 'context')]
where the time goes in v1:
time: 730 us; the launch traced here: 728 us
  waiting for transfers between devices  528 us (72%)
  matrix products  54.2 us (7%)
  local copies, waits for them, and re-layouts  50.2 us (7%)
  blocking collectives  44.7 us (6%)
  other arithmetic  34.8 us (5%)
  between operations  15.2 us (2%)
    all_gather x1, waiting for transfers between devices, on_device(): packed = jnp.sum(lax.all_gather(packed, 'context'), axis=0)  124 us
    reduce_scatter x1, waiting for transfers between devices, on_device(): lax.psum_scatter(back_result[2].astype(jnp.bfloat16), 'context', scatter_...  74.7 us
    reduce_scatter x1, waiting for transfers between devices, on_device(): lax.psum_scatter(back_result[1].astype(jnp.bfloat16), 'context', scatter_...  67.5 us
    reduce_scatter x1, waiting for transfers between devices, on_device(): packed = lax.psum_scatter(packed, 'fsdp', scatter_dimension=0, tiled=True)  62.2 us
    all_gather x1, waiting for transfers between devices, on_device(): lax.all_gather(value_flat, 'context', axis=0, tiled=True)  42.2 us
    psum x1, waiting for transfers between devices, on_device(): lax.psum(jnp.dot(gate_up_grad, gelu_flat.T, preferred_element_type=jnp.fl...  41.8 us
    psum x1, waiting for transfers between devices, on_device(): residual = inputs + lax.psum(attn_part, 'tensor')  40.8 us
    all_gather x1, waiting for transfers between devices, on_device(): lax.all_gather(key_flat, 'context', axis=0, tiled=True)  33.9 us
  transfers between devices with their start and end apart: 11, of which 11 were waited for; matrix products, arithmetic and copies ran while one was open for 7% of the time, Pallas kernels for 0%

profile of v1, /device:TPU:0, one launch (start us, length us, event | category | flops | bytes accessed | tf_op | source)
XLA Modules:
  0.0 728.2 jit_solution(14247577715995963772)
XLA Ops:
  11.6 14.7 %all-reduce.2 = (bf16[768]{0:T(1024)(128)(2,1)S(1)}, bf16[768]{0:T(1024)(128)(2,1)S(1)}) all-reduce(bf16[768]{0:T(1024)(128)(2,1)S(1)} %dynamic-update-slice, bf16[768]{0:T(1024)(128)(2,1)S(1)} %dynamic-update-slice.1), channel_id=1, replica_groups=mesh['fsdp'=8,'tensor'=2,'context'=8] {'fsdp'}, use_global_device_ids=true, to_apply=%add | all-reduce | flops 1536 | bytes 6144
  30.6 6.5 all-gather.7.cloned.1.call-done
  37.1 2.6 copy.51
  42.6 1.7 slice.139
  45.6 13.2 %all_gather.36 = bf16[384,768]{0,1:T(8,128)(2,1)S(1)} all-gather(bf16[384,96]{0,1:T(8,128)(2,1)S(1)} %copy-done.46), channel_id=1, replica_groups=mesh['fsdp'=8,'tensor'=2,'context'=8] {'fsdp'}, dimensions={1}, use_global_device_ids=true | all-gather | bytes 663552 | tf_op jit(solution)/shard_map/all_gather | solution.py:119
  58.8 33.9 %all-gather.11.cloned.1.call-done = bf16[2048,384]{0,1:T(8,128)(2,1)} async-done(((bf16[256,384]{0,1:T(8,128)(2,1)}), bf16[2048,384]{0,1:T(8,128)(2,1)}) %all-gather.11.cloned.1.call-update) | async-done | bytes 1572880 | tf_op jit(solution)/shard_map/all_gather | solution.py:144
  92.7 3.9 select_reduce_fusion.1
  96.6 3.9 select_reduce_fusion
  101.1 42.2 %all-gather.9.cloned.1.call-done = bf16[2048,384]{0,1:T(8,128)(2,1)} async-done(((bf16[256,384]{0,1:T(8,128)(2,1)}), bf16[2048,384]{0,1:T(8,128)(2,1)}) %all-gather.9.cloned.1.call-update) | async-done | bytes 1572880 | tf_op jit(solution)/shard_map/all_gather | solution.py:145
  143.3 7.7 %fusion.13 = bf16[6,64,256]{2,1,0:T(8,128)(2,1)S(1)} fusion(bf16[2048,6,64]{0,2,1:T(8,128)(2,1)} %bitcast.186, f32[6,256,2048]{2,1,0:T(8,128)} %copy-done.7, f32[6,256]{1,0:T(8,128)S(1)} %log_add_fusion, pred[256,2048]{1,0:T(8,128)(4,1)S(1)} %broadcast_compare_fusion.1), kind=kOutput, calls=%fused_computation.37 | convolution fusion | flops 415334400 | bytes 14882816 | tf_op jit(solution)/shard_map/hqk,khd->qhd/dot_general | solution.py:162
  151.0 1.3 fusion.52
  152.4 16.8 %all_gather.39 = bf16[576,768]{0,1:T(8,128)(2,1)} all-gather(bf16[576,96]{0,1:T(8,128)(2,1)S(1)} %copy-done.45), channel_id=1, replica_groups=mesh['fsdp'=8,'tensor'=2,'context'=8] {'fsdp'}, dimensions={1}, use_global_device_ids=true | all-gather | bytes 995328 | tf_op jit(solution)/shard_map/all_gather | solution.py:121
  170.0 2.7 copy.53
  172.7 40.8 %all-reduce.8.cloned.1.call-done = f32[256,768]{1,0:T(8,128)} async-done(((f32[256,768]{1,0:T(8,128)}), f32[256,768]{1,0:T(8,128)}) %all-reduce.8.cloned.1.call-update) | async-done | bytes 786448 | tf_op jit(solution)/shard_map/psum | solution.py:167
  213.5 1.4 fusion.49
  217.8 1.7 convolution_bitcast_fusion.1
  219.8 41.8 %all-reduce.10.cloned.1.call-done = f32[256,768]{1,0:T(8,128)} async-done(((f32[256,768]{1,0:T(8,128)}), f32[256,768]{1,0:T(8,128)}) %all-reduce.10.cloned.1.call-update) | async-done | bytes 786448 | tf_op jit(solution)/shard_map/psum | solution.py:191
  261.6 2.1 multiply_reduce_fusion
  263.8 1.4 multiply_add_fusion
  266.4 2.1 broadcast.210
  268.5 2.0 broadcast.210.clone
  270.5 40.4 %while.20 = (s32[]{:T(128)}, f32[256,6,64]{0,2,1:T(8,128)}, f32[2048,384]{0,1:T(8,128)}, f32[2048,384]{0,1:T(8,128)}, bf16[2048,384]{0,1:T(8,128)(2,1)}, /*index...) while((s32[]{:T(128)}, f32[256,6,64]{0,2,1:T(8,128)}, ...), condition=%wide.region_19.20_spmd.clone, body=%wide.region_17.19_spmd.clone.sunk | while | flops 1024107520 | bytes 131182336 | solution.py:84
  273.2 1.8 constant_dynamic-slice_fusion.5
  275.0 3.3 fusion.105
  278.4 2.6 fusion.106
  281.0 4.3 fusion.107
  288.1 1.7 copy-done.3
  293.4 1.8 constant_dynamic-slice_fusion.5
  295.2 3.3 fusion.105
  298.6 2.7 fusion.106
  301.2 4.3 fusion.107
  308.3 1.7 copy-done.3
  310.9 3.4 convert_element_type.160
  314.4 1.4 convert_element_type.161
  317.6 1.3 convolution_convert_fusion.1
  318.9 2.7 fusion.48
  321.6 67.5 %reduce-scatter.4.cloned.1.call-done = bf16[256,384]{0,1:T(8,128)(2,1)} async-done(((bf16[2048,384]{0,1:T(8,128)(2,1)}), bf16[256,384]{0,1:T(8,128)(2,1)}) %reduce-scatter.4.cloned.1.call-update) | async-done | bytes 196624 | tf_op jit(solution)/shard_map/reduce_scatter | solution.py:278
  391.1 74.7 %reduce-scatter.6.cloned.1.call-done = bf16[256,384]{0,1:T(8,128)(2,1)} async-done(((bf16[2048,384]{0,1:T(8,128)(2,1)}), bf16[256,384]{0,1:T(8,128)(2,1)}) %reduce-scatter.6.cloned.1.call-update) | async-done | bytes 196624 | tf_op jit(solution)/shard_map/reduce_scatter | solution.py:281
  467.6 1.5 convolution_convert_fusion
  469.1 3.0 convolution_bitcast_fusion
  472.3 1.4 fusion.38
  473.7 2.6 fusion.45
  476.3 32.8 %all-reduce.12.cloned.1.call-done = (bf16[256,768]{1,0:T(8,128)(2,1)}, bf16[256,768]{1,0:T(8,128)(2,1)}) async-done(((bf16[256,768]{1,0:T(8,128)(2,1)}, bf16[256,768]{1,0:T(8,128)(2,1)}), (bf16[256,768]{1,0:T(8,128)(2,1)}, bf16[256,768]{1,0:T(8,128)(2,1)})) %all-reduce.12.cloned.1.call-update) | async-done | bytes 786448 | tf_op jit(solution)/shard_map/psum | solution.py:179
  509.1 1.4 fusion.27
  510.7 13.5 %concatenate.21 = f32[768,3266]{1,0:T(8,128)} concatenate(f32[768,1]{1,0:T(8,128)S(1)} %broadcast_in_dim.141, f32[768,1]{1,0:T(8,128)S(1)} %broadcast_in_dim.142, f32[768,1152]{1,0:T(8,128)} %fusion.45, f32[768,1152]{1,0:T(8,128)} %fusion.48, f32[768,384]{1,0:T(8,128)} %fusion.38, f32[768,576]{1,0:T(8,128)} %convolution_bitcast_fusion), dimensions={1} | concatenate | bytes 20066304 | tf_op jit(solution)/shard_map/concatenate | solution.py:317
  524.3 62.2 %reduce-scatter.8.cloned.1.call-done = f32[96,3266]{1,0:T(8,128)} async-done(((f32[768,3266]{1,0:T(8,128)}), f32[96,3266]{1,0:T(8,128)}) %reduce-scatter.8.cloned.1.call-update) | async-done | bytes 1254160 | tf_op jit(solution)/shard_map/reduce_scatter | solution.py:318
  588.6 124.0 %all-gather.15.cloned.1.call-done = f32[768,3266]{1,0:T(8,128)} async-done(((f32[96,3266]{1,0:T(8,128)}), f32[768,3266]{1,0:T(8,128)}) %all-gather.15.cloned.1.call-update) | async-done | bytes 10033168 | tf_op jit(solution)/shard_map/all_gather | solution.py:319
  712.6 4.6 reduce_sum.174
  (249 shorter events, 42.8 us)
Async XLA Ops:
  7.2 32.6 %copy-start.10 = (bf16[256,768]{1,0:T(8,128)(2,1)S(1)}, bf16[256,768]{1,0:T(8,128)(2,1)}, u32[]{:S(2)}) copy-start(bf16[256,768]{1,0:T(8,128)(2,1)} %param.11) | copy-start | bytes 1179652
  7.2 29.9 %all-gather.7.cloned.1.call-start = ((), (), s32[]{:S(2)}) async-start(), calls=%async_computation.3 | async-start | bytes 1990656 | tf_op jit(solution)/shard_map/all_gather | solution.py:118
  7.9 84.8 %all-gather.11.cloned.1.call-start = ((), (), s32[]{:S(2)}) async-start(), calls=%async_computation.5 | async-start | bytes 1769472 | tf_op jit(solution)/shard_map/all_gather | solution.py:144
  30.3 10.2 %copy-start.50 = (f32[256]{0:T(256)}, f32[256]{0:T(256)S(1)}, u32[]{:S(2)}) copy-start(f32[256]{0:T(256)S(1)} %add_rsqrt_fusion.1) | copy-start | bytes 3076
  30.6 11.1 %copy-start.40 = (f32[256,32]{0,1:T(8,128)}, f32[256,32]{0,1:T(8,128)S(1)}, u32[]{:S(2)}) copy-start(f32[256,32]{0,1:T(8,128)S(1)} %get-tuple-element.409) | copy-start | bytes 98308
  30.6 11.1 %copy-start.41 = (f32[256,32]{0,1:T(8,128)}, f32[256,32]{0,1:T(8,128)S(1)}, u32[]{:S(2)}) copy-start(f32[256,32]{0,1:T(8,128)S(1)} %get-tuple-element.410) | copy-start | bytes 98308
  39.7 4.6 copy-start.44
  41.6 4.1 copy-start.46
  41.8 54.8 %copy-start.33 = (bf16[256,6,32]{0,2,1:T(8,128)(2,1)}, bf16[256,6,32]{0,2,1:T(8,128)(2,1)S(1)}, u32[]{:S(2)}) copy-start(bf16[256,6,32]{0,2,1:T(8,128)(2,1)S(1)} %get-tuple-element.401) | copy-start | bytes 294916
  41.8 54.8 %copy-start.35 = (bf16[256,6,32]{0,2,1:T(8,128)(2,1)}, bf16[256,6,32]{0,2,1:T(8,128)(2,1)S(1)}, u32[]{:S(2)}) copy-start(bf16[256,6,32]{0,2,1:T(8,128)(2,1)S(1)} %get-tuple-element.402) | copy-start | bytes 294916
  42.5 100.8 %all-gather.9.cloned.1.call-start = ((), (), s32[]{:S(2)}) async-start(), calls=%async_computation.4 | async-start | bytes 1769472 | tf_op jit(solution)/shard_map/all_gather | solution.py:145
  44.3 125.7 %all-gather.13.cloned.1.call-start = ((), (), s32[]{:S(2)}) async-start(), calls=%async_computation.7 | async-start | bytes 2211840 | tf_op jit(solution)/shard_map/all_gather | solution.py:120
  45.1 168.4 %all-reduce.8.cloned.1.call-start = ((), (), s32[]{:S(2)}) async-start(), calls=%async_computation.6 | async-start | bytes 1572864 | tf_op jit(solution)/shard_map/psum | solution.py:167
  58.8 92.1 %copy-start.19 = (bf16[384,768]{0,1:T(8,128)(2,1)}, bf16[384,768]{0,1:T(8,128)(2,1)S(1)}, u32[]{:S(2)}) copy-start(bf16[384,768]{0,1:T(8,128)(2,1)S(1)} %all_gather.36) | copy-start | bytes 1769476
  96.6 4.5 copy-start.7
  101.1 49.8 %copy-start.58 = (f32[6,256]{1,0:T(8,128)}, f32[6,256]{1,0:T(8,128)S(1)}, u32[]{:S(2)}) copy-start(f32[6,256]{1,0:T(8,128)S(1)} %log_add_fusion) | copy-start | bytes 18436
  143.3 9.1 %copy-start.45 = (bf16[576,96]{0,1:T(8,128)(2,1)S(1)}, bf16[576,96]{0,1:T(8,128)(2,1)}, u32[]{:S(2)}) copy-start(bf16[576,96]{0,1:T(8,128)(2,1)} %param.18) | copy-start | bytes 331780
  152.3 109.3 %all-reduce.10.cloned.1.call-start = ((), (), s32[]{:S(2)}) async-start(), calls=%async_computation.8 | async-start | bytes 1572864 | tf_op jit(solution)/shard_map/psum | solution.py:191
  172.7 44.1 %copy-start.31 = (bf16[256,768]{1,0:T(8,128)(2,1)S(1)}, bf16[256,768]{1,0:T(8,128)(2,1)}, u32[]{:S(2)}) copy-start(bf16[256,768]{1,0:T(8,128)(2,1)} %param.19) | copy-start | bytes 1179652
  214.9 48.9 %copy-start.8 = (f32[256,768]{1,0:T(8,128)}, f32[256,768]{1,0:T(8,128)S(1)}, u32[]{:S(2)}) copy-start(f32[256,768]{1,0:T(8,128)S(1)} %get-tuple-element.388) | copy-start | bytes 2359300
  217.5 46.2 %copy-start.42 = (bf16[256,1,576]{0,2,1:T(8,128)(2,1)}, bf16[256,1,576]{0,2,1:T(8,128)(2,1)S(1)}, u32[]{:S(2)}) copy-start(bf16[256,1,576]{0,2,1:T(8,128)(2,1)S(1)} %get-tuple-element.391) | copy-start | bytes 884740
  217.5 46.2 %copy-start.43 = (bf16[256,1,576]{0,2,1:T(8,128)(2,1)}, bf16[256,1,576]{0,2,1:T(8,128)(2,1)S(1)}, u32[]{:S(2)}) copy-start(bf16[256,1,576]{0,2,1:T(8,128)(2,1)S(1)} %get-tuple-element.392) | copy-start | bytes 884740
  217.5 44.1 %copy-start.48 = (f32[256]{0:T(256)S(1)}, f32[256]{0:T(256)}, u32[]{:S(2)}) copy-start(f32[256]{0:T(256)} %copy-done.47) | copy-start | bytes 3076
  217.5 44.1 %copy-start.53 = (f32[256]{0:T(256)S(1)}, f32[256]{0:T(256)}, u32[]{:S(2)}) copy-start(f32[256]{0:T(256)} %copy-done.52) | copy-start | bytes 3076
  217.8 45.9 %copy-start.32 = (bf16[256,768]{1,0:T(8,128)(2,1)S(1)}, bf16[256,768]{1,0:T(8,128)(2,1)}, u32[]{:S(2)}) copy-start(bf16[256,768]{1,0:T(8,128)(2,1)} %param.19) | copy-start | bytes 1179652
  219.6 45.6 %copy-start.20 = (bf16[384,768]{0,1:T(8,128)(2,1)S(1)}, bf16[384,768]{0,1:T(8,128)(2,1)}, u32[]{:S(2)}) copy-start(bf16[384,768]{0,1:T(8,128)(2,1)} %copy-done.19) | copy-start | bytes 1769476
  219.6 169.6 %reduce-scatter.4.cloned.1.call-start = ((), (), s32[]{:S(2)}) async-start(), calls=%async_computation.9 | async-start | bytes 1769472 | tf_op jit(solution)/shard_map/reduce_scatter | solution.py:278
  265.2 5.4 copy-start.15
  272.9 5.5 copy-start.1
  273.2 5.2 copy-start.17
  281.0 5.4 copy-start.4
  293.0 5.5 copy-start.1
  293.4 5.2 copy-start.17
  301.2 5.4 copy-start.4
  310.9 3.5 copy-start.6
  314.4 151.4 %reduce-scatter.6.cloned.1.call-start = ((), (), s32[]{:S(2)}) async-start(), calls=%async_computation.10 | async-start | bytes 1769472 | tf_op jit(solution)/shard_map/reduce_scatter | solution.py:281
  315.9 193.2 %all-reduce.12.cloned.1.call-start = ((), (), s32[]{:S(2)}) async-start(), calls=%async_computation.13 | async-start | bytes 1572864 | tf_op jit(solution)/shard_map/psum | solution.py:179
  318.9 71.2 %copy-start.14 = (f32[256,6,64]{0,2,1:T(8,128)S(1)}, f32[256,6,64]{0,2,1:T(8,128)}, u32[]{:S(2)}) copy-start(f32[256,6,64]{0,2,1:T(8,128)} %get-tuple-element.285) | copy-start | bytes 1179652
  318.9 148.7 %copy-start.13 = (bf16[768,3,384]{0,2,1:T(8,128)(2,1)S(1)}, bf16[768,3,384]{0,2,1:T(8,128)(2,1)}, u32[]{:S(2)}) copy-start(bf16[768,3,384]{0,2,1:T(8,128)(2,1)} %copy-done.12) | copy-start | bytes 5308420
  466.8 5.3 copy-start.55
  467.6 4.7 copy-start.16
  469.0 4.7 copy-start.11
  469.0 4.7 copy-start.22
  469.0 4.7 copy-start.51
  469.1 117.4 %reduce-scatter.8.cloned.1.call-start = ((), (), s32[]{:S(2)}) async-start(), calls=%async_computation.11 | async-start | bytes 11501568 | tf_op jit(solution)/shard_map/reduce_scatter | solution.py:318
  524.2 62.3 %copy-start.39 = (bf16[256,768]{1,0:T(8,128)(2,1)S(1)}, bf16[256,768]{1,0:T(8,128)(2,1)}, u32[]{:S(2)}) copy-start(bf16[256,768]{1,0:T(8,128)(2,1)} %get-tuple-element.385) | copy-start | bytes 1179652
  524.2 63.2 %copy-start.30 = (bf16[256,768]{1,0:T(8,128)(2,1)S(1)}, bf16[256,768]{1,0:T(8,128)(2,1)}, u32[]{:S(2)}) copy-start(bf16[256,768]{1,0:T(8,128)(2,1)} %get-tuple-element.386) | copy-start | bytes 1179652
  524.3 188.3 %all-gather.15.cloned.1.call-start = ((), (), s32[]{:S(2)}) async-start(), calls=%async_computation.12 | async-start | bytes 11501568 | tf_op jit(solution)/shard_map/all_gather | solution.py:319
  (41 other events, 95.8 us)
Sparse Core Ops, SparseCore 0:
  9.7 27.3 all-gather.6
  42.7 50.0 all-gather.10
  95.5 47.7 all-gather.8
  145.4 24.5 all-gather.12
  172.8 40.5 all-reduce.7
  219.7 41.8 all-reduce.9
  314.5 74.6 reduce-scatter.3
  393.3 72.4 reduce-scatter.5
  469.2 39.8 all-reduce.11
  524.4 62.0 reduce-scatter.7
  589.1 123.4 all-gather.14
